TPU v7x, 128 devices: a whole 4x4x4 slice. The times are simulated.
128 devices in a mesh: tm: 4 (over z), chan: 32 (over x, y, core).
Axes of the slice: x: 4, y: 4, z: 4, core: 2. Of those that a mesh axis runs over, the one named last changes fastest.
Arguments:
- phase_step: float32 [8, 256, 131072], P(None, 'tm', 'chan'), may hold values from -3.1416 to 3.1416, as said below
- wrap_count: int32 [8, 256, 131072], P(None, 'tm', 'chan'), may hold values from -1 to 1
- coupling: float32 [8], replicated, may hold values from 0.5 to 2
- filter_taps: float32 [8, 128], replicated, may hold values from -0.06 to 0.06
Outputs:
- strain: float32 [8, 256, 131072], P(None, 'tm', 'chan')
Inputs may be any that keep to these rules, and one draw needn't show every extreme that they name: `phase_step`: wrapped phase differences, within -pi to pi.
All inputs are finite; a program needn't handle non-finite values.
Results may differ from a plain program's by a relative error of at most 0.00007.
Values sent between devices are 32-bit elements; how exact they have to be, the bound alone decides.
A program may use at most 128 MiB of HBM per device.

v0:
```python
import math

import jax
import jax.numpy as jnp
from jax import lax
from jax.sharding import PartitionSpec as P

two_pi = 2.0 * math.pi


def from_everyone(shard, axis):
    copies = jnp.broadcast_to(shard, (lax.axis_size(axis), *shard.shape))
    return lax.all_to_all(copies, axis, split_axis=0, concat_axis=0, tiled=True)


def laid_out(pieces, dim):
    pieces = jnp.moveaxis(pieces, 0, dim)
    lengths = pieces.shape
    return pieces.reshape(*lengths[:dim], lengths[dim] * lengths[dim + 1], *lengths[dim + 2 :])


def gathered_copies(shard, axis, dim):
    pieces = from_everyone(shard, axis)
    return laid_out(pieces, dim)


def of_everyone(shard, axis):
    everything = from_everyone(shard, axis)
    return jnp.sum(everything, axis=0)


def extended(block, sides, width):
    for axis, dim in sides:
        count = lax.axis_size(axis)
        forward = [(i, i + 1) for i in range(count - 1)]
        backward = [(target, source) for source, target in forward]
        low = lax.ppermute(
            lax.slice_in_dim(block, block.shape[dim] - width, None, axis=dim), axis, forward
        )
        high = lax.ppermute(lax.slice_in_dim(block, 0, width, axis=dim), axis, backward)
        block = jnp.concatenate([low, block, high], axis=dim)
    return block


def spatial_filter(padded, filter_taps):
    stacked = jnp.transpose(padded, (1, 0, 2))
    kernel = filter_taps[:, None, :]
    result = lax.conv_general_dilated(
        stacked,
        kernel,
        (1,),
        "VALID",
        feature_group_count=filter_taps.shape[0],
        precision=lax.Precision.HIGHEST,
    )
    return jnp.transpose(result, (1, 0, 2))


def earlier_blocks(totals, position):
    gathered = gathered_copies(totals[None], "tm", 0)
    earlier_mask = (jnp.arange(gathered.shape[0]) < position).astype(jnp.float32)
    return jnp.sum(gathered * earlier_mask[:, None, None], axis=0)


def shards(phase_step, wrap_count, coupling, filter_taps):
    increment = phase_step + two_pi * wrap_count.astype(jnp.float32)
    partial_value = jnp.cumsum(increment, axis=1)
    block_total = partial_value[:, -1, :]
    position = lax.axis_index("tm")
    width = phase_step.shape[2]
    half = filter_taps.shape[1] // 2
    offset = earlier_blocks(block_total, position)
    unwrapped = partial_value + offset[:, None, :]
    population = phase_step.shape[0] * width * lax.axis_size("chan")
    mode_sums = of_everyone(jnp.sum(unwrapped, axis=(0, 2)), "chan")
    common = mode_sums / population
    shifted = coupling[:, None, None] * common[None, :, None]
    leveled = unwrapped - shifted
    padded = extended(leveled, (("chan", 2),), half)
    filtered = spatial_filter(padded, filter_taps)[:, :, :width]
    return (leveled - filtered) * (1.0 / (4.0 * two_pi))


def solution(mesh):
    placed = (P(None, "tm", "chan"), P(None, "tm", "chan"), P(), P())
    return jax.shard_map(
        shards, mesh=mesh, in_specs=placed, out_specs=P(None, "tm", "chan"), check_vma=False
    )
```

profile of v0, /device:TPU:1, one launch (start us, length us, event | category | flops | bytes accessed | tf_op | source)
XLA Modules:
  0.0 704.6 jit_solution(9353079562583257612)
XLA Ops:
  0.0 11.7 %multiply_add_fusion = f32[8,64,4096]{2,1,0:T(8,128)} fusion(f32[8,64,4096]{2,1,0:T(8,128)} %param.4, s32[8,64,4096]{2,1,0:T(8,128)} %param.5), kind=kLoop, calls=%fused_computation.11 | loop fusion | flops 6291456 | bytes 25165824 | tf_op jit(solution)/shard_map/add | solution.py:66
  11.7 11.5 %fusion.8 = f32[8,64,4096]{2,0,1:T(8,128)} fusion(f32[8,64,4096]{2,1,0:T(8,128)} %multiply_add_fusion), kind=kOutput, calls=%fused_computation.9 | output fusion | flops 132120576 | bytes 16777216 | tf_op jit(solution)/shard_map/jit(cumsum)/reduce_window_sum | solution.py:67
  23.2 0.9 slice_bitcast_fusion
  24.1 0.8 broadcast_in_dim.6
  24.9 5.8 all-to-all-start
  30.8 13.4 %copy.16 = f32[8,64,4096]{1,0,2:T(8,128)} copy(f32[8,64,4096]{2,0,1:T(8,128)} %fusion.8) | data formatting | bytes 16777216 | tf_op jit(solution)/shard_map/jit(cumsum)/reduce_window_sum | solution.py:67
  44.2 0.0 copy-start.2
  44.2 0.0 all-to-all-done
  44.2 0.1 fusion.10
  44.3 0.6 copy.15
  44.9 7.7 %add_reduce_fusion = f32[64]{0:T(128)S(1)} fusion(f32[8,64,4096]{1,0,2:T(8,128)} %copy.16, f32[8,4096]{0,1:T(8,128)S(1)} %copy.15), kind=kLoop, calls=%fused_computation.8 | loop fusion | flops 4194240 | bytes 8519936 | tf_op jit(solution)/shard_map/reduce_sum | solution.py:75
  52.6 14.8 %all_to_all.11 = f32[32,1,64]{2,1,0:T(1,128)S(1)} all-to-all(f32[32,1,64]{2,1,0:T(1,128)S(1)} %broadcast_in_dim.14), channel_id=1, replica_groups=mesh['tm'=4,'chan'=32] {'chan'}, dimensions={0} | all-to-all | bytes 16384 | tf_op jit(solution)/shard_map/all_to_all | solution.py:13
  67.4 0.0 copy-done.2
  67.4 0.1 broadcast_multiply_fusion
  67.5 0.0 copy-start.1
  67.5 11.1 %add_subtract_fusion = f32[8,64,4096]{1,0,2:T(8,128)S(1)} fusion(f32[8,64,4096]{1,0,2:T(8,128)} %copy.16, f32[8,64]{1,0:T(8,128)S(1)} %broadcast_multiply_fusion, f32[8,4096]{0,1:T(8,128)S(1)} %copy.15), kind=kLoop, calls=%fused_computation.7 | loop fusion | flops 4194304 | bytes 16910336 | tf_op jit(solution)/shard_map/sub | solution.py:78
  78.6 0.0 copy-start
  78.6 5.7 copy-done
  84.4 2.7 collective-permute-start
  87.1 2.1 collective-permute-start.1
  89.2 0.0 copy-done.1
  89.2 0.1 copy.18
  89.3 1.1 collective-permute-done
  90.4 4.4 collective-permute-done.1
  94.8 11.0 %fusion.17 = f32[8,64,4224]{1,0,2:T(8,128)S(1)} fusion(f32[8,64,64]{1,0,2:T(8,128)S(1)} %collective-permute-done.1, f32[8,64,4096]{1,0,2:T(8,128)} %copy-done, f32[8,64,64]{1,0,2:T(8,128)S(1)} %collective-permute-done), kind=kLoop, calls=%fused_computation.1.clone.clone.clone.1 | loop fusion | flops 4325376 | bytes 17301504 | tf_op jit(solution)/shard_map/slice | solution.py:80
  105.8 586.0 %subtract_multiply_fusion = f32[8,64,4096]{1,0,2:T(8,128)} fusion(f32[8,64,4096]{1,0,2:T(8,128)} %copy-done, f32[8,1,128]{0,1,2:T(1,128)S(1)} %copy.18, f32[8,64,4224]{1,0,2:T(8,128)S(1)} %fusion.17), kind=kOutput, calls=%fused_computation.6 | convolution fusion | flops 3225419776 | bytes 25432064 | tf_op jit(solution)/shard_map/slice | solution.py:80
  691.9 12.7 %copy.19 = f32[8,64,4096]{2,1,0:T(8,128)} copy(f32[8,64,4096]{1,0,2:T(8,128)} %subtract_multiply_fusion) | data formatting | bytes 16777216 | tf_op jit(solution)/shard_map/mul | solution.py:81
  (5 shorter events, 0.1 us)
Async XLA Ops:
  24.9 19.2 %all-to-all-start = ((f32[4,1,8,4096]{3,2,1,0:T(8,128)}), f32[4,1,8,4096]{3,2,1,0:T(8,128)S(1)}, u32[]{:S(2)}, u32[]{:S(2)}) async-start(f32[4,1,8,4096]{3,2,1,0:T(8,128)} %broadcast_in_dim.6), calls=%async_computation | async-start | bytes 1048576 | tf_op jit(solution)/shard_map/all_to_all | solution.py:13
  44.2 23.3 %copy-start.2 = (f32[8]{0:T(128)S(1)}, f32[8]{0:T(128)}, u32[]{:S(2)}) copy-start(f32[8]{0:T(128)} %param.6) | copy-start | bytes 100
  67.5 21.7 %copy-start.1 = (f32[8,128]{1,0:T(8,128)S(1)}, f32[8,128]{1,0:T(8,128)}, u32[]{:S(2)}) copy-start(f32[8,128]{1,0:T(8,128)} %param.7) | copy-start | bytes 12292
  78.6 5.7 copy-start
  84.4 6.0 collective-permute-start
  87.1 7.7 %collective-permute-start.1 = (f32[8,64,64]{1,0,2:T(8,128)S(1)}, f32[8,64,64]{1,0,2:T(8,128)S(1)}, u32[]{:S(2)}, u32[]{:S(2)}) collective-permute-start(f32[8,64,64]{1,0,2:T(8,128)S(1)} %get-tuple-element.6), channel_id=1, source_target_pairs={{1,0},{2,1},{3,2},{4,3},{5,4},{6,5},{7,6},{8,7},{9,8},{10,9},{11,1... | collective-permute-start | bytes 393224 | tf_op jit(solution)/shard_map/ppermute | solution.py:40
where the time goes:
time: 706 us; the launch traced here: 705 us
  matrix products  586 us (83%)
  other arithmetic  53.2 us (8%)
  local copies, waits for them, and re-layouts  34.3 us (5%)
  blocking collectives  14.8 us (2%)
  starting transfers between devices  10.7 us (2%)
    slice x1, matrix products, shards(): filtered = spatial_filter(padded, filter_taps)[:, :, :width]  586 us
    all_to_all x1, blocking collectives, from_everyone(): return lax.all_to_all(copies, axis, split_axis=0, concat_axis=0, tiled=True)  14.8 us
  transfers between devices with their start and end apart: 3, of which 2 were waited for; matrix products, arithmetic and copies ran while one was open for 2% of the time, Pallas kernels for 0%

commit v1 on v0

v1 whole, which is shorter than its diff:
```python
import functools
import math

import jax
import jax.numpy as jnp
from jax import lax
from jax.experimental import pallas as pl
from jax.experimental.pallas import tpu as pltpu
from jax.sharding import PartitionSpec as P

two_pi = 2.0 * math.pi
scale = 1.0 / (4.0 * two_pi)
LANES = 128
GROUP = 8
f32 = jnp.float32
bf16 = jnp.bfloat16


def halves(x):
    high = x.astype(bf16)
    return high, (x - high.astype(f32)).astype(bf16)


def running_sum(rows, sublane):
    for shift in (1, 2, 4):
        turned = [pltpu.roll(row, shift, 0) for row in rows]
        wraps = sublane < shift
        summed = []
        for i, row in enumerate(rows):
            above = turned[i - 1] if i else jnp.zeros_like(row)
            summed.append(row + jnp.where(wraps, above, turned[i]))
        rows = summed
    for i in range(1, len(rows)):
        rows[i] = rows[i] + rows[i - 1]
    return rows


def main_kernel(
    n_tm, n_chan,
    phase, wrap, coupling, taps,
    y_hbm, offset_out, edge_out, common_out,
    pbuf, wbuf, zhi, zlo, ybuf, matrix, sums, ends,
    send_left, send_right, halo_left, halo_right,
    ends_in, far_send, far_in, own_row, row_in, plane_row, plane_in,
    sem_in, sem_out, sem_edge,
    s_left, s_right, r_left, r_right,
    s_ends, r_ends, s_far, r_far, s_row, r_row, s_plane, r_plane,
):
    cables, times, width = phase.shape
    blocks = width // LANES
    groups = blocks // GROUP
    parts = times // 16
    tm = lax.axis_index("tm")
    chan = lax.axis_index("chan")

    def load(c):
        return (
            pltpu.make_async_copy(phase.at[c], pbuf.at[c], sem_in.at[0, c]),
            pltpu.make_async_copy(wrap.at[c], wbuf.at[c], sem_in.at[1, c]),
        )

    for c in range(cables):
        for copy in load(c):
            copy.start()

    barrier = pltpu.get_barrier_semaphore()

    @pl.loop(1, n_chan)
    def _(d):
        pl.semaphore_signal(barrier, inc=1, device_id={"chan": lax.rem(chan + d, n_chan)})

    for d in range(1, n_tm):
        pl.semaphore_signal(barrier, inc=1, device_id={"tm": lax.rem(tm + d, n_tm)})

    lane = lax.broadcasted_iota(jnp.int32, (1, 2 * LANES), 1)

    @pl.loop(0, cables)
    def _(c):
        row = (jnp.where(lane == LANES // 2, 1.0, 0.0) - taps[c]) * scale
        row = jnp.where(lane < LANES, row, 0.0)
        high = row.astype(bf16).astype(f32)
        for i, part in enumerate((high, row - high)):
            spread = jnp.broadcast_to(part, (LANES, 2 * LANES))
            turned = pltpu.roll(spread, 0, 1, stride=1, stride_axis=0)
            matrix[c, :, i * LANES : (i + 1) * LANES] = turned.T.astype(bf16)

    sublane = lax.broadcasted_iota(jnp.int32, (8, LANES), 0)
    sums[...] = jnp.zeros_like(sums)

    @pl.when(chan == 0)
    def _():
        halo_left[...] = jnp.zeros_like(halo_left)

    @pl.when(chan == n_chan - 1)
    def _():
        halo_right[...] = jnp.zeros_like(halo_right)

    pl.semaphore_wait(barrier, n_chan - 1 + n_tm - 1)

    def to_left(c):
        return pltpu.make_async_remote_copy(
            send_left.at[c], halo_right.at[c], s_left.at[c], r_right.at[c],
            device_id={"chan": chan - 1},
        )

    def to_right(c):
        return pltpu.make_async_remote_copy(
            send_right.at[c], halo_left.at[c], s_right.at[c], r_left.at[c],
            device_id={"chan": chan + 1},
        )

    def later(d, src, dst, send, recv):
        return pltpu.make_async_remote_copy(
            src, dst, send, recv, device_id={"tm": tm + d}
        )

    def ends_to(d, c):
        return later(d, ends.at[c], ends_in.at[tm, c], s_ends.at[d - 1, c], r_ends.at[d - 1, c])

    def far_to(d):
        return later(d, far_send, far_in.at[tm], s_far.at[d - 1], r_far.at[d - 1])

    def row_to(d):
        return later(d, own_row, row_in.at[tm], s_row.at[d - 1], r_row.at[d - 1])

    def for_later(action):
        for d in range(1, n_tm):
            pl.when(tm + d < n_tm)(functools.partial(action, d))

    def from_earlier(action):
        for d in range(1, n_tm):
            pl.when(tm - d >= 0)(functools.partial(action, d))

    def accumulate(c, g):
        total = [None] * (times // 8)
        for b in range(GROUP):
            block = g * GROUP + b
            col = pl.multiple_of(block * LANES, LANES)
            rows = []
            for i in range(times // 8):
                step = pbuf[c, 8 * i : 8 * i + 8, pl.ds(col, LANES)]
                turns = wbuf[c, 8 * i : 8 * i + 8, pl.ds(col, LANES)]
                rows.append(step + two_pi * turns.astype(f32))
            rows = running_sum(rows, sublane)
            for i, row in enumerate(rows):
                total[i] = row if total[i] is None else total[i] + row
            ends[c, pl.ds(block, 1), :] = rows[-1][7:8, :]
            if b == 0:
                slot = jnp.where(g == 0, c, cables)
                for i, row in enumerate(rows):
                    send_left[slot, 8 * i : 8 * i + 8, :] = row
            if b == GROUP - 1:
                slot = jnp.where(g == groups - 1, c, cables)
                for i, row in enumerate(rows):
                    send_right[slot, 8 * i : 8 * i + 8, :] = row
            for i in range(parts):
                x = jnp.concatenate(rows[2 * i : 2 * i + 2], axis=0)
                high, low = halves(x)
                zhi[c, i, block + 1] = high
                zlo[c, i, block + 1] = low
        for i, row in enumerate(total):
            sums[8 * i : 8 * i + 8, :] += row

    @pl.loop(0, cables)
    def _(c):
        for copy in load(c):
            copy.wait()

        @pl.loop(0, groups)
        def _(g):
            accumulate(c, g)

        @pl.when(chan > 0)
        def _():
            to_left(c).start()

        @pl.when(chan < n_chan - 1)
        def _():
            to_right(c).start()

        for_later(lambda d: ends_to(d, c).start())

    both = jnp.concatenate([sums[...], jnp.zeros_like(sums)], axis=0)
    own_row[...] = jnp.sum(both.T, axis=0, keepdims=True)
    for_later(lambda d: row_to(d).start())

    def window(z, c, w):
        return jnp.concatenate(
            [jnp.concatenate([z[c, i, w], z[c, i, w + 1]], axis=1) for i in range(parts)],
            axis=0,
        )

    def push(c):
        for mxu in range(2):
            pltpu.matmul_push_rhs(matrix[c], 0, mxu)

    def joined(pair):
        return pair[:, :LANES] + pair[:, LANES:]

    def interior(c, g):
        def body(*acc):
            push(c)
            for b in range(GROUP):
                w = g * GROUP + b
                pltpu.matmul_acc_lhs(acc[b], window(zhi, c, w), 0 if b < 2 else None)
                pltpu.matmul_acc_lhs(acc[b], window(zlo, c, w))
            for b in range(GROUP):
                col = pl.multiple_of((g * GROUP + b) * LANES, LANES)
                ybuf[c, :, pl.ds(col, LANES)] = joined(pltpu.matmul_pop(acc[b]))

        pl.run_scoped(body, *[pltpu.ACC(b % 2)((times, 2 * LANES), f32) for b in range(GROUP)])

    def middle_out(c):
        return pltpu.make_async_copy(
            ybuf.at[c, :, pl.ds(LANES, width - LANES)],
            y_hbm.at[c, :, pl.ds(LANES, width - LANES)],
            sem_out.at[c],
        )

    def edges_out(c):
        return [
            pltpu.make_async_copy(
                ybuf.at[c, :, pl.ds(col, LANES)], y_hbm.at[c, :, pl.ds(col, LANES)], sem_edge.at[i, c]
            )
            for i, col in enumerate((0, width))
        ]

    def to_plane(d):
        return pltpu.make_async_remote_copy(
            plane_row, plane_in.at[chan], s_plane.at[d], r_plane.at[d],
            device_id={"chan": lax.rem(chan + d, n_chan)},
        )

    def relay():
        from_earlier(lambda d: row_to(d).wait_recv())
        row = own_row[...]
        for source in range(n_tm - 1):
            last = row_in[source][:, times - 1 : times]
            row = row + jnp.where(source < tm, last, 0.0)
        plane_row[...] = row
        plane_in[chan] = row

        @pl.loop(1, n_chan)
        def _(d):
            to_plane(d).start()

        @pl.when(chan > 0)
        def _():
            @pl.loop(0, cables)
            def _(c):
                to_right(c).wait_recv()

        @pl.when(chan < n_chan - 1)
        def _():
            @pl.loop(0, cables)
            def _(c):
                to_left(c).wait_recv()

        for c in range(cables):
            far_send[c : c + 1, :] = halo_left[c, times - 1 : times, :]
            far_send[cables + c : cables + c + 1, :] = halo_right[c, times - 1 : times, :]
        for_later(lambda d: far_to(d).start())

    @pl.loop(0, cables)
    def _(c):
        pl.when(c == 2)(relay)

        @pl.loop(0, groups)
        def _(g):
            interior(c, g)

        middle_out(c).start()

    @pl.loop(0, cables)
    def _(c):
        from_earlier(lambda d: ends_to(d, c).wait_recv())

    from_earlier(lambda d: far_to(d).wait_recv())
    far = jnp.zeros_like(far_send)
    for source in range(n_tm - 1):
        far = far + jnp.where(source < tm, far_in[source], 0.0)
    far_send_sum = far
    far_rows = far_send_sum

    position = lax.broadcasted_iota(jnp.int32, (48, LANES), 0)
    ones = jnp.ones((16, LANES), f32)
    which = lax.broadcasted_iota(jnp.int32, (16, LANES), 0)
    no_left = jnp.where(which == 1, 0.0, ones).astype(bf16)
    no_right = jnp.where(which == 2, 0.0, ones).astype(bf16)
    one_rows = jnp.concatenate([no_left, no_right], axis=1)

    for c in range(cables):
        for i in range(parts):
            for halo, at in ((halo_left, 0), (halo_right, blocks + 1)):
                high, low = halves(halo[c, 16 * i : 16 * i + 16, :])
                zhi[c, i, at] = high
                zlo[c, i, at] = low
        earlier = jnp.zeros((blocks, LANES), f32)
        for source in range(n_tm - 1):
            earlier = earlier + jnp.where(source < tm, ends_in[source, c], 0.0)
        tail = jnp.zeros((48 - blocks, LANES), f32)
        here = jnp.concatenate([earlier, tail], axis=0)
        before = pltpu.roll(here, 1, 0)
        before = jnp.where(position == 0, far_rows[c : c + 1, :], before)
        here = jnp.where(position == blocks, far_rows[cables + c : cables + c + 1, :], here)

        def body(first, last, small, constant):
            push(c)
            for k, z in enumerate((zhi, zlo)):
                pltpu.matmul_acc_lhs(first, window(z, c, 0), None if k else 0)
                pltpu.matmul_acc_lhs(last, window(z, c, blocks), None if k else 0)
            before_parts, here_parts = halves(before), halves(here)
            for x, y in zip(before_parts, here_parts):
                pltpu.matmul_acc_lhs(small, jnp.concatenate([x, y], axis=1))
            pltpu.matmul_acc_lhs(constant, one_rows)
            ybuf[c, :, 0:LANES] = joined(pltpu.matmul_pop(first))
            ybuf[c, :, width : width + LANES] = joined(pltpu.matmul_pop(last))
            offset_out[c] = joined(pltpu.matmul_pop(small))
            flat = joined(pltpu.matmul_pop(constant))
            flat = flat * coupling[c]
            edge = jnp.broadcast_to(flat[0:1, :], (48, LANES))
            edge = jnp.where((position == 0) & (chan == 0), flat[1:2, :], edge)
            edge = jnp.where((position == blocks) & (chan == n_chan - 1), flat[2:3, :], edge)
            edge_out[c] = edge

        pl.run_scoped(
            body,
            pltpu.ACC(0)((times, 2 * LANES), f32),
            pltpu.ACC(1)((times, 2 * LANES), f32),
            pltpu.ACC(0)((48, 2 * LANES), f32),
            pltpu.ACC(1)((16, 2 * LANES), f32),
        )
        for copy in edges_out(c):
            copy.start()

    @pl.loop(1, n_chan)
    def _(d):
        to_plane(d).wait_recv()

    row = jnp.sum(plane_in[...], axis=0) * (1.0 / (cables * width * n_chan))
    common_out[...] = jnp.broadcast_to(row, (LANES, LANES)).T[:times]

    @pl.loop(1, n_chan)
    def _(d):
        to_plane(d).wait_send()

    for_later(lambda d: row_to(d).wait_send())
    for_later(lambda d: far_to(d).wait_send())

    @pl.loop(0, cables)
    def _(c):
        for_later(lambda d: ends_to(d, c).wait_send())

        @pl.when(chan > 0)
        def _():
            to_left(c).wait_send()

        @pl.when(chan < n_chan - 1)
        def _():
            to_right(c).wait_send()

        middle_out(c).wait()
        for copy in edges_out(c):
            copy.wait()


def final_kernel(y, offset, edge, common, out):
    times = common.shape[0]
    blocks = out.shape[2] // LANES
    left = lax.broadcasted_iota(jnp.int32, (times, LANES), 1) < LANES // 2
    before = None
    for w in range(blocks + 1):
        v = y[0, :, w * LANES : (w + 1) * LANES] + (
            offset[0, w : w + 1, :] - common[...] * edge[0, w : w + 1, :]
        )
        v = pltpu.roll(v, LANES // 2, 1)
        if w:
            out[0, :, (w - 1) * LANES : w * LANES] = jnp.where(left, before, v)
        before = v


def shards(phase_step, wrap_count, coupling, filter_taps):
    cables, times, width = phase_step.shape
    blocks = width // LANES
    n_tm, n_chan = lax.axis_size("tm"), lax.axis_size("chan")
    taps = jnp.pad(filter_taps, ((0, 0), (0, LANES)))[:, None, :]
    vmem, dma = pltpu.VMEM, pltpu.SemaphoreType.DMA
    full = (cables, times, width)
    edge = (cables + 1, times, LANES)
    z = (cables, times // 16, blocks + 2, 16, LANES)
    small = jax.ShapeDtypeStruct((cables, 48, LANES), f32)
    y, offset, edges, common = pl.pallas_call(
        functools.partial(main_kernel, n_tm, n_chan),
        out_shape=(
            jax.ShapeDtypeStruct((cables, times, width + LANES), f32),
            small,
            small,
            jax.ShapeDtypeStruct((times, LANES), f32),
        ),
        in_specs=[
            pl.BlockSpec(memory_space=pl.ANY),
            pl.BlockSpec(memory_space=pl.ANY),
            pl.BlockSpec(memory_space=pltpu.SMEM),
            pl.BlockSpec(memory_space=vmem),
        ],
        out_specs=(
            pl.BlockSpec(memory_space=pl.ANY),
            pl.BlockSpec(memory_space=vmem),
            pl.BlockSpec(memory_space=vmem),
            pl.BlockSpec(memory_space=vmem),
        ),
        scratch_shapes=[
            vmem(full, f32), vmem(full, jnp.int32), vmem(z, bf16), vmem(z, bf16),
            vmem((cables, times, width + LANES), f32),
            vmem((cables, 2 * LANES, 2 * LANES), bf16),
            vmem((times, LANES), f32), vmem((cables, blocks, LANES), f32),
            vmem(edge, f32), vmem(edge, f32),
            vmem((cables, times, LANES), f32), vmem((cables, times, LANES), f32),
            vmem((n_tm, cables, blocks, LANES), f32),
            vmem((2 * cables, LANES), f32), vmem((n_tm, 2 * cables, LANES), f32),
            vmem((1, LANES), f32), vmem((n_tm, 1, LANES), f32),
            vmem((1, LANES), f32), vmem((n_chan, 1, LANES), f32),
            dma((2, cables)), dma((cables,)), dma((2, cables)),
            dma((cables,)), dma((cables,)), dma((cables,)), dma((cables,)),
            dma((n_tm - 1, cables)), dma((n_tm - 1, cables)),
            dma((n_tm - 1,)), dma((n_tm - 1,)),
            dma((n_tm - 1,)), dma((n_tm - 1,)),
            dma((n_chan,)), dma((n_chan,)),
        ],
        compiler_params=pltpu.CompilerParams(
            collective_id=0, has_side_effects=True, vmem_limit_bytes=60 << 20
        ),
        name="level",
    )(phase_step, wrap_count, coupling, taps)
    return pl.pallas_call(
        final_kernel,
        grid=(cables,),
        out_shape=jax.ShapeDtypeStruct(full, f32),
        in_specs=[
            pl.BlockSpec((1, times, width + LANES), lambda c: (c, 0, 0)),
            pl.BlockSpec((1, 48, LANES), lambda c: (c, 0, 0)),
            pl.BlockSpec((1, 48, LANES), lambda c: (c, 0, 0)),
            pl.BlockSpec((times, LANES), lambda c: (0, 0)),
        ],
        out_specs=pl.BlockSpec((1, times, width), lambda c: (c, 0, 0)),
        name="finish",
    )(y, offset, edges, common)


def solution(mesh):
    placed = (P(None, "tm", "chan"), P(None, "tm", "chan"), P(), P())
    return jax.shard_map(
        shards, mesh=mesh, in_specs=placed, out_specs=P(None, "tm", "chan"), check_vma=False
    )
```

time: 706 us -> 39.5 us (0.06)
  matrix products: 586 us -> 0 us
  other arithmetic: 53.2 us -> 0 us
  Pallas kernels: 0 us -> 37.8 us
  local copies, waits for them, and re-layouts: 34.3 us -> 1.29 us
  blocking collectives: 14.8 us -> 0 us
  starting transfers between devices: 10.7 us -> 0 us
    slice x1 -> x0, matrix products: 586 us -> none  [shards(): filtered = spatial_filter(padded, filter_taps)[:, :, :width]]
    pallas_call x0 -> x2, Pallas kernels: none -> 37.8 us  [the longest x1 27.7 us: shards(): pl.pallas_call(functools.partial(main_kernel, n_tm, n_chan), out_shape=(j...]
    all_to_all x1 -> x0, blocking collectives: 14.8 us -> none  [from_everyone(): return lax.all_to_all(copies, axis, split_axis=0, concat_axis=0, tiled=True)]
    another operation x2 -> x0, local copies, waits for them, and re-layouts: 14.3 us -> none  [the longest x1 13.4 us: shards(): partial_value = jnp.cumsum(increment, axis=1)]
    mul x1 -> x0, local copies, waits for them, and re-layouts: 12.7 us -> none  [shards(): return (leveled - filtered) * (1.0 / (4.0 * two_pi))]
    add x1 -> x0, other arithmetic: 11.7 us -> none  [shards(): increment = phase_step + two_pi * wrap_count.astype(jnp.float32)]
    another operation x1 -> x0, other arithmetic: 11.5 us -> none  [shards(): partial_value = jnp.cumsum(increment, axis=1)]
    sub x1 -> x0, other arithmetic: 11.1 us -> none  [shards(): leveled = unwrapped - shifted]
  transfers between devices with their start and end apart: 3 -> 0, of which waited for: 2 -> 0; matrix products, arithmetic and copies ran while one was open for 2% -> 0% of each run, Pallas kernels for 0% -> 0%
where the time goes in v1:
time: 39.5 us; the launch traced here: 39.1 us
  Pallas kernels  37.8 us (96%)
  local copies, waits for them, and re-layouts  1.29 us (3%)
    pallas_call x1, Pallas kernels, shards(): pl.pallas_call(functools.partial(main_kernel, n_tm, n_chan), out_shape=(j...  27.7 us
    pallas_call x1, Pallas kernels, shards(): pl.pallas_call(final_kernel, grid=(cables,), out_shape=jax.ShapeDtypeStru...  10.1 us

profile of v1, /device:TPU:1, one launch (start us, length us, event | category | flops | bytes accessed | tf_op | source)
XLA Modules:
  0.0 39.1 jit_solution(11725345712214630511)
XLA Ops:
  0.0 0.7 %pad.4 = f32[8,256]{1,0:T(8,128)S(1)} pad(f32[8,128]{1,0:T(8,128)} %param.7, f32[]{:T(128)} %constant.2.clone.1), padding=0_0x0_128 | pad | bytes 12292 | tf_op jit(solution)/shard_map/jit(_pad)/pad | solution.py:386
  0.7 0.6 %broadcast_in_dim.3.taps = f32[8,1,256]{2,1,0:T(1,128)} reshape(f32[8,256]{1,0:T(8,128)S(1)} %pad.4) | data formatting | bytes 16384 | tf_op jit(solution)/shard_map/broadcast_in_dim | solution.py:386
  1.3 27.7 %level.1 = (f32[8,64,4224]{2,1,0:T(8,128)}, f32[8,48,128]{2,1,0:T(8,128)}, f32[8,48,128]{2,1,0:T(8,128)}, f32[64,128]{1,0:T(8,128)}) custom-call(f32[8,64,4096]{2,1,0:T(8,128)} %phase.1, s32[8,64,4096]{2,1,0:T(8,128)} %wrap.1, f32[8]{0:T(128)} %coupling.1, f32[8,1,256]{2,1,0:T(1,128)} %broadcast_in_dim.3.taps), custom_call_target="tpu_custom_call" | custom-call | tf_op jit(solution)/shard_map/level/pallas_call | solution.py:392
  29.0 10.1 %finish.1 = f32[8,64,4096]{2,1,0:T(8,128)} custom-call(f32[8,64,4224]{2,1,0:T(8,128)} %get-tuple-element.9.y, f32[8,48,128]{2,1,0:T(8,128)} %get-tuple-element.10.offset, f32[8,48,128]{2,1,0:T(8,128)} %get-tuple-element.11.edge, f32[64,128]{1,0:T(8,128)} %get-tuple-element.12.common), custom_call_target="tpu_custom_call" | custom-call | tf_op jit(solution)/shard_map/finish/pallas_call | solution.py:435

commit v2 on v1

v2 whole, which is shorter than its diff:
```python
import functools
import math

import jax
import jax.numpy as jnp
from jax import lax
from jax.experimental import pallas as pl
from jax.experimental.pallas import tpu as pltpu
from jax.sharding import PartitionSpec as P

two_pi = 2.0 * math.pi
scale = 1.0 / (4.0 * two_pi)
LANES = 128
GROUP = 11
RING = 8
RELAY = 3
LIMIT = 48
f32 = jnp.float32
bf16 = jnp.bfloat16


def halves(x):
    high = x.astype(bf16)
    return high, (x - high.astype(f32)).astype(bf16)


def running_sum(rows, sublane):
    rows = list(rows)
    for k in range(1, len(rows)):
        rows[k] = rows[k] + rows[k - 1]
    before = rows[-1]
    for shift in (1, 2, 4):
        before = before + jnp.where(sublane >= shift, pltpu.roll(before, shift, 0), 0.0)
    before = jnp.where(sublane >= 1, pltpu.roll(before, 1, 0), 0.0)
    return [row + before for row in rows]


def main_kernel(
    n_tm, n_chan,
    phase, wrap, coupling, taps,
    ybuf, offset_out, edge_out, common_out,
    pbuf, wbuf, zhi, zlo, swap_in, swap_out, carry, matrix, sums, ends,
    send_left, send_right, halo_left, halo_right,
    ends_in, far_send, far_in, own_row, row_in, plane_row, plane_in,
    sem_in, s_left, s_right, r_left, r_right,
    s_ends, r_ends, s_far, r_far, s_row, r_row, s_plane, r_plane,
):
    cables, times, width = phase.shape
    blocks = width // LANES
    groups = (blocks + 1) // GROUP
    assert groups * GROUP == blocks + 1 and times == 64
    parts = times // 16
    tm = lax.axis_index("tm")
    chan = lax.axis_index("chan")

    def load(c):
        return (
            pltpu.make_async_copy(phase.at[c], pbuf.at[c, :, pl.ds(0, width)], sem_in.at[0, c]),
            pltpu.make_async_copy(wrap.at[c], wbuf.at[c, :, pl.ds(0, width)], sem_in.at[1, c]),
        )

    for c in range(cables):
        for copy in load(c):
            copy.start()

    barrier = pltpu.get_barrier_semaphore()

    @pl.loop(1, n_chan)
    def _(d):
        pl.semaphore_signal(barrier, inc=1, device_id={"chan": chan ^ d})

    for d in range(1, n_tm):
        pl.semaphore_signal(barrier, inc=1, device_id={"tm": tm ^ d})

    lane = lax.broadcasted_iota(jnp.int32, (1, LANES), 1)

    @pl.loop(0, cables)
    def _(c):
        row = (jnp.where(lane == LANES // 2, 1.0, 0.0) - taps[pl.ds(c, 1), :]) * scale
        row = jnp.concatenate([row, jnp.zeros_like(row)], axis=1)
        high = row.astype(bf16).astype(f32)
        for i, part in enumerate((high, row - high)):
            spread = jnp.broadcast_to(part, (LANES, 2 * LANES))
            turned = pltpu.roll(spread, 0, 1, stride=1, stride_axis=0)
            matrix[c, i * LANES : (i + 1) * LANES, :] = turned.astype(bf16)

    sublane = lax.broadcasted_iota(jnp.int32, (8, LANES), 0)
    left = lax.broadcasted_iota(jnp.int32, (8, LANES), 1) < LANES // 2
    sums[...] = jnp.zeros_like(sums)
    ends[:, blocks:, :] = jnp.zeros((cables, 8, LANES), f32)

    @pl.when(chan == 0)
    def _():
        halo_left[...] = jnp.zeros_like(halo_left)

    @pl.when(chan == n_chan - 1)
    def _():
        halo_right[...] = jnp.zeros_like(halo_right)

    pl.semaphore_wait(barrier, n_chan - 1 + n_tm - 1)

    def to_left(c):
        return pltpu.make_async_remote_copy(
            send_left.at[c], halo_right.at[c], s_left.at[c], r_right.at[c],
            device_id={"chan": chan - 1},
        )

    def to_right(c):
        return pltpu.make_async_remote_copy(
            send_right.at[c], halo_left.at[c], s_right.at[c], r_left.at[c],
            device_id={"chan": chan + 1},
        )

    def later(d, src, dst, send, recv):
        return pltpu.make_async_remote_copy(src, dst, send, recv, device_id={"tm": tm + d})

    def ends_to(d, src, dst):
        return later(d, src, dst, s_ends.at[d - 1], r_ends.at[d - 1])

    def far_to(d):
        return later(d, far_send, far_in.at[tm], s_far.at[d - 1], r_far.at[d - 1])

    def row_to(d):
        return later(d, own_row, row_in.at[tm], s_row.at[d - 1], r_row.at[d - 1])

    def for_later(action):
        for d in range(1, n_tm):
            pl.when(tm + d < n_tm)(functools.partial(action, d))

    def from_earlier(action):
        for d in range(1, n_tm):
            pl.when(tm - d >= 0)(functools.partial(action, d))

    def put(c, at, rows):
        for i in range(parts):
            high, low = halves(jnp.concatenate(rows[2 * i : 2 * i + 2], axis=0))
            zhi[c, i, at] = high
            zlo[c, i, at] = low

    def turn(row):
        return pltpu.roll(row, LANES // 2, 1)

    def accumulate(c, g):
        total = [None] * 8
        final = g == groups - 1
        previous = [jnp.where(g == 0, 0.0, carry[8 * i : 8 * i + 8, :]) for i in range(8)]
        for b in range(GROUP):
            block = g * GROUP + b
            col = pl.ds(pl.multiple_of(block * LANES, LANES), LANES)
            for i in range(8):
                at = slice(8 * i, 8 * i + 8)
                turned = turn(pbuf[c, at, col] + two_pi * wbuf[c, at, col].astype(f32))
                if b == GROUP - 1:
                    turned = jnp.where(final, 0.0, turned)
                swap_in[b][pl.ds(25 * i, 8, stride=3), :] = jnp.where(left, previous[i], turned)
                previous[i] = turned
            rows = running_sum(
                [swap_in[b][pl.ds(3 * k, 8, stride=25), :] for k in range(8)], sublane
            )
            for k, row in enumerate(rows):
                swap_out[b][pl.ds(3 * k, 8, stride=25), :] = row
            rows = [swap_out[b][pl.ds(25 * i, 8, stride=3), :] for i in range(8)]
            for i, row in enumerate(rows):
                total[i] = row if total[i] is None else total[i] + row
            ends[c, pl.ds(block, 1), :] = rows[-1][7:8, :]
            if b == 0:
                slot = jnp.where(g == 0, c, cables)
                for i, row in enumerate(rows):
                    send_left[slot, 8 * i : 8 * i + 8, :] = row
            if b == GROUP - 1:
                slot = jnp.where(final, c, cables)
                for i, row in enumerate(rows):
                    send_right[slot, 8 * i : 8 * i + 8, :] = row
            put(c, block, rows)
        for i, row in enumerate(total):
            sums[8 * i : 8 * i + 8, :] += row
            carry[8 * i : 8 * i + 8, :] = previous[i]

    @pl.loop(0, cables)
    def _(c):
        for copy in load(c):
            copy.wait()

        @pl.loop(0, groups)
        def _(g):
            accumulate(c, g)

        @pl.when(chan > 0)
        def _():
            to_left(c).start()

        @pl.when(chan < n_chan - 1)
        def _():
            to_right(c).start()

        for_later(lambda d: ends_to(d, ends.at[c], ends_in.at[tm, c]).start())

    both = jnp.concatenate([sums[...], jnp.zeros_like(sums)], axis=0)
    own_row[...] = jnp.sum(both.T, axis=0, keepdims=True)
    for_later(lambda d: row_to(d).start())

    def window(z, c, w):
        return jnp.concatenate(
            [jnp.concatenate([z[c, i, w], z[c, i, w + 1]], axis=1) for i in range(parts)],
            axis=0,
        )

    def push(c):
        for mxu in range(2):
            pltpu.matmul_push_rhs(matrix[c], 0, mxu, transpose=True)

    def joined(acc):
        pair = pltpu.matmul_pop(acc)
        return pair[:, :LANES] + pair[:, LANES:]

    def filtered(c, acc):
        push(c)
        order = [*range(1, blocks - 1), 0, blocks - 1]

        def finish(n):
            col = order[n] * LANES
            ybuf[c, :, col : col + LANES] = joined(acc[n % RING])

        for n, w in enumerate(order):
            if n >= RING:
                finish(n - RING)
            pltpu.matmul_acc_lhs(acc[n % RING], window(zhi, c, w), 0 if n < 2 else None)
            pltpu.matmul_acc_lhs(acc[n % RING], window(zlo, c, w))
        for n in range(blocks - RING, blocks):
            finish(n)

    def to_plane(d):
        return pltpu.make_async_remote_copy(
            plane_row, plane_in.at[chan], s_plane, r_plane, device_id={"chan": chan ^ d}
        )

    def all_plane():
        others = plane_in.at[pl.ds(0, n_chan - 1)]
        return pltpu.make_async_remote_copy(
            others, others, s_plane, r_plane, device_id={"chan": chan ^ 1}
        )

    def relay_row():
        from_earlier(lambda d: row_to(d).wait_recv())
        row = own_row[...]
        for source in range(n_tm - 1):
            last = row_in[source][:, times - 1 : times]
            row = row + jnp.where(source < tm, last, 0.0)
        plane_row[...] = row
        plane_in[chan] = row

        @pl.loop(1, n_chan)
        def _(d):
            to_plane(d).start()

    def halos(c):
        @pl.when(chan > 0)
        def _():
            to_right(c).wait_recv()

        @pl.when(chan < n_chan - 1)
        def _():
            to_left(c).wait_recv()

    def relay_far():
        pl.loop(RELAY, cables)(halos)
        inner = left[:1]
        for c in range(cables):
            last = slice(times - 1, times)
            far_send[c : c + 1, :] = jnp.where(inner, halo_left[c, last, :], 0.0)
            far_send[cables + c : cables + c + 1, :] = jnp.where(inner, 0.0, halo_right[c, last, :])
        for_later(lambda d: far_to(d).start())

    @pl.loop(0, cables)
    def _(c):
        @pl.when(c == RELAY)
        def _():
            relay_row()
            relay_far()

        @pl.when(c < RELAY)
        def _():
            halos(c)

        def tile(buffer, i):
            return buffer[c, 8 * i : 8 * i + 8, :]

        for at, low, high in ((0, halo_left, send_left), (blocks, send_right, halo_right)):
            put(c, at, [jnp.where(left, tile(low, i), tile(high, i)) for i in range(8)])
        pl.run_scoped(
            lambda *acc: filtered(c, acc),
            *[pltpu.ACC(n % 2)((times, 2 * LANES), f32) for n in range(RING)],
        )

    from_earlier(lambda d: ends_to(d, ends, ends_in.at[tm]).wait_recv())
    from_earlier(lambda d: far_to(d).wait_recv())
    far = jnp.zeros_like(far_send)
    for source in range(n_tm - 1):
        far = far + jnp.where(source < tm, far_in[source], 0.0)

    padded = blocks + 8
    row_of = lax.broadcasted_iota(jnp.int32, (padded, LANES), 0)
    position = row_of[:blocks]
    ones = jnp.ones((16, LANES), f32)
    which = lax.broadcasted_iota(jnp.int32, (16, LANES), 0)
    half = lax.broadcasted_iota(jnp.int32, (16, LANES), 1) < LANES // 2
    one_rows = jnp.concatenate(
        [
            jnp.where((which == 1) & half, 0.0, ones).astype(bf16),
            jnp.where((which == 2) & ~half, 0.0, ones).astype(bf16),
        ],
        axis=1,
    )

    def constants(*accs):
        for c in range(cables):
            mxu, small, constant = c % 2, accs[2 * c], accs[2 * c + 1]
            here = jnp.zeros((padded, LANES), f32)
            for source in range(n_tm - 1):
                here = here + jnp.where(source < tm, ends_in[source, c], 0.0)
            here = here + jnp.where(row_of == 0, far[c : c + 1, :], 0.0)
            here = here + jnp.where(row_of == blocks, far[cables + c : cables + c + 1, :], 0.0)
            after = pltpu.roll(here, padded - 1, 0)[:blocks]
            pltpu.matmul_push_rhs(matrix[c], 0, mxu, transpose=True)
            for i, pair in enumerate(zip(halves(here[:blocks]), halves(after))):
                pltpu.matmul_acc_lhs(small, jnp.concatenate(pair, axis=1), None if i else 0)
            pltpu.matmul_acc_lhs(constant, one_rows)
        for c in range(cables):
            offset_out[c] = joined(accs[2 * c])
            flat = joined(accs[2 * c + 1]) * coupling[c]
            edge = jnp.broadcast_to(flat[0:1, :], (blocks, LANES))
            edge = jnp.where((position == 0) & (chan == 0), flat[1:2, :], edge)
            edge = jnp.where((position == blocks - 1) & (chan == n_chan - 1), flat[2:3, :], edge)
            edge_out[c] = edge

    pl.run_scoped(
        constants,
        *[
            pltpu.ACC(c % 2)((size, 2 * LANES), f32)
            for c in range(cables)
            for size in (blocks, 16)
        ],
    )

    for_later(lambda d: row_to(d).wait_send())
    for_later(lambda d: far_to(d).wait_send())
    for_later(lambda d: ends_to(d, ends, ends_in.at[tm]).wait_send())

    @pl.loop(0, cables)
    def _(c):
        @pl.when(chan > 0)
        def _():
            to_left(c).wait_send()

        @pl.when(chan < n_chan - 1)
        def _():
            to_right(c).wait_send()

    all_plane().wait_send()
    all_plane().wait_recv()
    row = jnp.sum(plane_in[...], axis=0) * (1.0 / (cables * blocks * LANES * n_chan))
    common_out[...] = jnp.broadcast_to(row, (LANES, LANES)).T[:times]


def final_kernel(y, offset, edge, common, out):
    c = pl.program_id(0)
    mode = common[...]
    for j in range(out.shape[2] // LANES):
        col = slice(j * LANES, (j + 1) * LANES)
        shift = offset[c, j : j + 1, :] - mode * edge[c, j : j + 1, :]
        out[0, :, col] = y[c, :, col] + shift


def shards(phase_step, wrap_count, coupling, filter_taps):
    cables, times, width = phase_step.shape
    blocks = width // LANES
    n_tm, n_chan = lax.axis_size("tm"), lax.axis_size("chan")
    vmem, dma = pltpu.VMEM, pltpu.SemaphoreType.DMA
    full = (cables, times, width)
    wide = (cables, times, width + LANES)
    edge = (cables + 1, times, LANES)
    z = (cables, times // 16, blocks + 1, 16, LANES)
    small = vmem((cables, blocks, LANES), f32)
    leveled = pl.pallas_call(
        functools.partial(main_kernel, n_tm, n_chan),
        out_shape=(
            vmem(full, f32),
            small,
            small,
            vmem((times, LANES), f32),
        ),
        in_specs=[
            pl.BlockSpec(memory_space=pl.ANY),
            pl.BlockSpec(memory_space=pl.ANY),
            pl.BlockSpec(memory_space=pltpu.SMEM),
            pl.BlockSpec(memory_space=vmem),
        ],
        out_specs=(
            pl.BlockSpec(memory_space=vmem),
            pl.BlockSpec(memory_space=vmem),
            pl.BlockSpec(memory_space=vmem),
            pl.BlockSpec(memory_space=vmem),
        ),
        scratch_shapes=[
            vmem(wide, f32), vmem(wide, jnp.int32), vmem(z, bf16), vmem(z, bf16),
            [vmem((200, LANES), f32)] * GROUP, [vmem((200, LANES), f32)] * GROUP, vmem((times, LANES), f32),
            vmem((cables, 2 * LANES, 2 * LANES), bf16),
            vmem((times, LANES), f32), vmem((cables, blocks + 8, LANES), f32),
            vmem(edge, f32), vmem(edge, f32),
            vmem((cables, times, LANES), f32), vmem((cables, times, LANES), f32),
            vmem((n_tm, cables, blocks + 8, LANES), f32),
            vmem((2 * cables, LANES), f32), vmem((n_tm, 2 * cables, LANES), f32),
            vmem((1, LANES), f32), vmem((n_tm, 1, LANES), f32),
            vmem((1, LANES), f32), vmem((n_chan, 1, LANES), f32),
            dma((2, cables)), dma((cables,)), dma((cables,)), dma((cables,)), dma((cables,)),
            dma((n_tm - 1,)), dma((n_tm - 1,)),
            dma((n_tm - 1,)), dma((n_tm - 1,)),
            dma((n_tm - 1,)), dma((n_tm - 1,)),
            dma, dma,
        ],
        compiler_params=pltpu.CompilerParams(
            collective_id=0, has_side_effects=True, vmem_limit_bytes=LIMIT << 20
        ),
        name="level",
    )(phase_step, wrap_count, coupling, filter_taps)
    return pl.pallas_call(
        final_kernel,
        grid=(cables,),
        out_shape=jax.ShapeDtypeStruct(full, f32),
        in_specs=[pl.BlockSpec(memory_space=vmem)] * 4,
        out_specs=pl.BlockSpec((1, times, width), lambda c: (c, 0, 0)),
        compiler_params=pltpu.CompilerParams(vmem_limit_bytes=16 << 20),
        name="finish",
    )(*[pltpu.with_memory_space_constraint(x, vmem) for x in leveled])


def solution(mesh):
    placed = (P(None, "tm", "chan"), P(None, "tm", "chan"), P(), P())
    return jax.shard_map(
        shards, mesh=mesh, in_specs=placed, out_specs=P(None, "tm", "chan"), check_vma=False
    )
```

time: 39.5 us -> 27.7 us (0.70)
  Pallas kernels: 37.8 us -> 27.5 us
  local copies, waits for them, and re-layouts: 1.29 us -> 0 us
    pallas_call x1, Pallas kernels: 10.1 us -> 4.73 us  [shards(): pl.pallas_call(final_kernel, grid=(cables,), out_shape=jax.ShapeDtypeStru...]
    pallas_call x1, Pallas kernels: 27.7 us -> 22.8 us  [shards(): pl.pallas_call(functools.partial(main_kernel, n_tm, n_chan), out_shape=(v...]
    pad x1 -> x0, local copies, waits for them, and re-layouts: 0.69 us -> none  [shards(): taps = jnp.pad(filter_taps, ((0, 0), (0, LANES)))[:, None, :]]
    broadcast_in_dim x1 -> x0, local copies, waits for them, and re-layouts: 0.61 us -> none  [shards(): taps = jnp.pad(filter_taps, ((0, 0), (0, LANES)))[:, None, :]]
where the time goes in v2:
time: 27.7 us; the launch traced here: 27.5 us
  Pallas kernels  27.5 us (99%)
    pallas_call x1, Pallas kernels, shards(): pl.pallas_call(functools.partial(main_kernel, n_tm, n_chan), out_shape=(v...  22.8 us
    pallas_call x1, Pallas kernels, shards(): pl.pallas_call(final_kernel, grid=(cables,), out_shape=jax.ShapeDtypeStru...  4.73 us

profile of v2, /device:TPU:1, one launch (start us, length us, event | category | flops | bytes accessed | tf_op | source)
XLA Modules:
  0.0 27.5 jit_solution(15846526811002855817)
XLA Ops:
  0.0 22.8 %level.1 = (f32[8,64,4096]{2,1,0:T(8,128)S(1)}, f32[8,32,128]{2,1,0:T(8,128)S(1)}, f32[8,32,128]{2,1,0:T(8,128)S(1)}, f32[64,128]{1,0:T(8,128)S(1)}) custom-call(f32[8,64,4096]{2,1,0:T(8,128)} %phase.1, s32[8,64,4096]{2,1,0:T(8,128)} %wrap.1, f32[8]{0:T(128)} %coupling.1, f32[8,128]{1,0:T(8,128)} %taps.1), custom_call_target="tpu_custom_call" | custom-call | tf_op jit(solution)/shard_map/level/pallas_call | solution.py:384
  22.8 4.7 %finish.1 = f32[8,64,4096]{2,1,0:T(8,128)} custom-call(f32[8,64,4096]{2,1,0:T(8,128)S(1)} %get-tuple-element.9.y, f32[8,32,128]{2,1,0:T(8,128)S(1)} %get-tuple-element.10.offset, f32[8,32,128]{2,1,0:T(8,128)S(1)} %get-tuple-element.11.edge, f32[64,128]{1,0:T(8,128)S(1)} %get-tuple-element.12.common), custom_call_target="tpu_custom_call" | custom-call | tf_op jit(solution)/shard_map/finish/pallas_call | solution.py:426

commit v3 on v2

--- a/solution.py
+++ b/solution.py
@@ -11,9 +11,12 @@
 two_pi = 2.0 * math.pi
 scale = 1.0 / (4.0 * two_pi)
 LANES = 128
-GROUP = 11
 RING = 8
-RELAY = 3
+CABLES = 2
+DEFER = 4
+RELAY = 2
+FAR_AT = 1
+FIRST = 20
 LIMIT = 48
 f32 = jnp.float32
 bf16 = jnp.bfloat16
@@ -39,7 +42,7 @@
     n_tm, n_chan,
     phase, wrap, coupling, taps,
     ybuf, offset_out, edge_out, common_out,
-    pbuf, wbuf, zhi, zlo, swap_in, swap_out, carry, matrix, sums, ends,
+    pbuf, wbuf, zhi, zlo, swap_in, swap_out, matrix, sums, late, ends,
     send_left, send_right, halo_left, halo_right,
     ends_in, far_send, far_in, own_row, row_in, plane_row, plane_in,
     sem_in, s_left, s_right, r_left, r_right,
@@ -47,8 +50,7 @@
 ):
     cables, times, width = phase.shape
     blocks = width // LANES
-    groups = (blocks + 1) // GROUP
-    assert groups * GROUP == blocks + 1 and times == 64
+    assert times == 64
     parts = times // 16
     tm = lax.axis_index("tm")
     chan = lax.axis_index("chan")
@@ -74,8 +76,7 @@
 
     lane = lax.broadcasted_iota(jnp.int32, (1, LANES), 1)
 
-    @pl.loop(0, cables)
-    def _(c):
+    def band(c):
         row = (jnp.where(lane == LANES // 2, 1.0, 0.0) - taps[pl.ds(c, 1), :]) * scale
         row = jnp.concatenate([row, jnp.zeros_like(row)], axis=1)
         high = row.astype(bf16).astype(f32)
@@ -84,6 +85,11 @@
             turned = pltpu.roll(spread, 0, 1, stride=1, stride_axis=0)
             matrix[c, i * LANES : (i + 1) * LANES, :] = turned.astype(bf16)
 
+    @pl.loop(0, cables, step=4)
+    def _(c):
+        for k in range(4):
+            band(c + k)
+
     sublane = lax.broadcasted_iota(jnp.int32, (8, LANES), 0)
     left = lax.broadcasted_iota(jnp.int32, (8, LANES), 1) < LANES // 2
     sums[...] = jnp.zeros_like(sums)
@@ -96,8 +102,6 @@
     @pl.when(chan == n_chan - 1)
     def _():
         halo_right[...] = jnp.zeros_like(halo_right)
-
-    pl.semaphore_wait(barrier, n_chan - 1 + n_tm - 1)
 
     def to_left(c):
         return pltpu.make_async_remote_copy(
@@ -140,51 +144,79 @@
     def turn(row):
         return pltpu.roll(row, LANES // 2, 1)
 
-    def accumulate(c, g):
-        total = [None] * 8
-        final = g == groups - 1
-        previous = [jnp.where(g == 0, 0.0, carry[8 * i : 8 * i + 8, :]) for i in range(8)]
-        for b in range(GROUP):
-            block = g * GROUP + b
-            col = pl.ds(pl.multiple_of(block * LANES, LANES), LANES)
+    def spread(c, b, previous, ready):
+        col = slice(b * LANES, (b + 1) * LANES)
+        for i in range(8):
+            at = slice(8 * i, 8 * i + 8)
+            if b < blocks:
+                step = pbuf[c, at, col]
+                if not ready:
+                    step = step + two_pi * wbuf[c, at, col].astype(f32)
+                turned = turn(step)
+            else:
+                turned = jnp.zeros((8, LANES), f32)
+            swap_in[b][pl.ds(25 * i, 8, stride=3), :] = jnp.where(left, previous[i], turned)
+            previous[i] = turned
+
+    def scan(b):
+        rows = [swap_in[b][pl.ds(3 * k, 8, stride=25), :] for k in range(8)]
+        for k, row in enumerate(running_sum(rows, sublane)):
+            swap_out[b][pl.ds(3 * k, 8, stride=25), :] = row
+
+    def scanned(b):
+        return [swap_out[b][pl.ds(25 * i, 8, stride=3), :] for i in range(8)]
+
+    def keep_edge(c, b, rows):
+        for edge, buffer in ((0, send_left), (blocks, send_right)):
+            if b == edge:
+                for i, row in enumerate(rows):
+                    buffer[c, 8 * i : 8 * i + 8, :] = row
+
+    def collect(c, b, total):
+        rows = scanned(b)
+        if total is not None:
+            for i, row in enumerate(rows):
+                total[i] = total[i] + row
+        ends[c, b : b + 1, :] = rows[-1][7:8, :]
+        if total is not None:
+            keep_edge(c, b, rows)
+        put(c, b, rows)
+
+    def accumulate(c, ready=False):
+        previous = [jnp.zeros((8, LANES), f32)] * 8
+        total = None if ready else [sums[8 * i : 8 * i + 8, :] for i in range(8)]
+        for b in range(blocks + 1):
+            spread(c, b, previous, ready)
+            scan(b)
+            collect(c, b, total)
+        if not ready:
+            for i, row in enumerate(total):
+                sums[8 * i : 8 * i + 8, :] = row
+
+    def edges(c):
+        spread(c, 0, [jnp.zeros((8, LANES), f32)] * 8, True)
+        spread(c, blocks, [turn(pbuf[c, 8 * i : 8 * i + 8, width - LANES : width]) for i in range(8)], True)
+        for b in (0, blocks):
+            scan(b)
+            keep_edge(c, b, scanned(b))
+
+    def increments(c):
+        total = [late[8 * i : 8 * i + 8, :] for i in range(8)]
+        for w in range(blocks):
+            col = slice(w * LANES, (w + 1) * LANES)
             for i in range(8):
                 at = slice(8 * i, 8 * i + 8)
-                turned = turn(pbuf[c, at, col] + two_pi * wbuf[c, at, col].astype(f32))
-                if b == GROUP - 1:
-                    turned = jnp.where(final, 0.0, turned)
-                swap_in[b][pl.ds(25 * i, 8, stride=3), :] = jnp.where(left, previous[i], turned)
-                previous[i] = turned
-            rows = running_sum(
-                [swap_in[b][pl.ds(3 * k, 8, stride=25), :] for k in range(8)], sublane
-            )
-            for k, row in enumerate(rows):
-                swap_out[b][pl.ds(3 * k, 8, stride=25), :] = row
-            rows = [swap_out[b][pl.ds(25 * i, 8, stride=3), :] for i in range(8)]
-            for i, row in enumerate(rows):
-                total[i] = row if total[i] is None else total[i] + row
-            ends[c, pl.ds(block, 1), :] = rows[-1][7:8, :]
-            if b == 0:
-                slot = jnp.where(g == 0, c, cables)
-                for i, row in enumerate(rows):
-                    send_left[slot, 8 * i : 8 * i + 8, :] = row
-            if b == GROUP - 1:
-                slot = jnp.where(final, c, cables)
-                for i, row in enumerate(rows):
-                    send_right[slot, 8 * i : 8 * i + 8, :] = row
-            put(c, block, rows)
+                step = pbuf[c, at, col] + two_pi * wbuf[c, at, col].astype(f32)
+                pbuf[c, at, col] = step
+                total[i] = total[i] + step
         for i, row in enumerate(total):
-            sums[8 * i : 8 * i + 8, :] += row
-            carry[8 * i : 8 * i + 8, :] = previous[i]
-
-    @pl.loop(0, cables)
-    def _(c):
+            late[8 * i : 8 * i + 8, :] = row
+
+    def arrived(c):
         for copy in load(c):
             copy.wait()
 
-        @pl.loop(0, groups)
-        def _(g):
-            accumulate(c, g)
-
+    def send_edges(c):
         @pl.when(chan > 0)
         def _():
             to_left(c).start()
@@ -193,51 +225,41 @@
         def _():
             to_right(c).start()
 
+    def send_ends(c):
         for_later(lambda d: ends_to(d, ends.at[c], ends_in.at[tm, c]).start())
+
+    @pl.loop(0, cables - DEFER)
+    def _(c):
+        arrived(c)
+        accumulate(c)
+
+    pl.semaphore_wait(barrier, n_chan - 1 + n_tm - 1)
+
+    pl.loop(0, cables - DEFER)(send_edges)
+
+    late[...] = jnp.zeros_like(late)
+
+    @pl.loop(cables - DEFER, cables)
+    def _(c):
+        arrived(c)
+        increments(c)
+        edges(c)
+        send_edges(c)
+
+    for i in range(8):
+        swap_in[0][pl.ds(25 * i, 8, stride=3), :] = late[8 * i : 8 * i + 8, :]
+    scan(0)
+    for i in range(8):
+        sums[8 * i : 8 * i + 8, :] += swap_out[0][pl.ds(25 * i, 8, stride=3), :]
 
     both = jnp.concatenate([sums[...], jnp.zeros_like(sums)], axis=0)
     own_row[...] = jnp.sum(both.T, axis=0, keepdims=True)
     for_later(lambda d: row_to(d).start())
-
-    def window(z, c, w):
-        return jnp.concatenate(
-            [jnp.concatenate([z[c, i, w], z[c, i, w + 1]], axis=1) for i in range(parts)],
-            axis=0,
-        )
-
-    def push(c):
-        for mxu in range(2):
-            pltpu.matmul_push_rhs(matrix[c], 0, mxu, transpose=True)
-
-    def joined(acc):
-        pair = pltpu.matmul_pop(acc)
-        return pair[:, :LANES] + pair[:, LANES:]
-
-    def filtered(c, acc):
-        push(c)
-        order = [*range(1, blocks - 1), 0, blocks - 1]
-
-        def finish(n):
-            col = order[n] * LANES
-            ybuf[c, :, col : col + LANES] = joined(acc[n % RING])
-
-        for n, w in enumerate(order):
-            if n >= RING:
-                finish(n - RING)
-            pltpu.matmul_acc_lhs(acc[n % RING], window(zhi, c, w), 0 if n < 2 else None)
-            pltpu.matmul_acc_lhs(acc[n % RING], window(zlo, c, w))
-        for n in range(blocks - RING, blocks):
-            finish(n)
+    pl.loop(0, cables - DEFER)(send_ends)
 
     def to_plane(d):
         return pltpu.make_async_remote_copy(
             plane_row, plane_in.at[chan], s_plane, r_plane, device_id={"chan": chan ^ d}
-        )
-
-    def all_plane():
-        others = plane_in.at[pl.ds(0, n_chan - 1)]
-        return pltpu.make_async_remote_copy(
-            others, others, s_plane, r_plane, device_id={"chan": chan ^ 1}
         )
 
     def relay_row():
@@ -248,10 +270,54 @@
             row = row + jnp.where(source < tm, last, 0.0)
         plane_row[...] = row
         plane_in[chan] = row
-
-        @pl.loop(1, n_chan)
-        def _(d):
-            to_plane(d).start()
+        for d in range(1, n_chan):
+            to_plane(d ^ FIRST if d != FIRST else FIRST).start()
+
+    @pl.loop(cables - DEFER, cables)
+    def _(c):
+        pl.when(c == cables - DEFER + RELAY)(relay_row)
+        accumulate(c, ready=True)
+        send_ends(c)
+
+    def window(z, c, w):
+        return jnp.concatenate(
+            [jnp.concatenate([z[c, i, w], z[c, i, w + 1]], axis=1) for i in range(parts)],
+            axis=0,
+        )
+
+    def push(c, register):
+        for mxu in range(2):
+            pltpu.matmul_push_rhs(matrix[c], register, mxu, transpose=True)
+
+    def joined(acc):
+        pair = pltpu.matmul_pop(acc)
+        return pair[:, :LANES] + pair[:, LANES:]
+
+    def filtered(first, acc):
+        order = [*range(1, blocks - 1), 0, blocks - 1]
+        work = [(first + k, w, n, k) for k in range(CABLES) for n, w in enumerate(order)]
+
+        def finish(m):
+            c, w, _, _ = work[m]
+            ybuf[c, :, w * LANES : (w + 1) * LANES] = joined(acc[m % RING])
+
+        push(first, 0)
+        for m, (c, w, n, k) in enumerate(work):
+            if m >= RING:
+                finish(m - RING)
+            fresh = k % 2 if n < 2 else None
+            pltpu.matmul_acc_lhs(acc[m % RING], window(zhi, c, w), fresh)
+            pltpu.matmul_acc_lhs(acc[m % RING], window(zlo, c, w))
+            if n == 2 and k + 1 < CABLES:
+                push(c + 1, (k + 1) % 2)
+        for m in range(len(work) - RING, len(work)):
+            finish(m)
+
+    def all_plane():
+        others = plane_in.at[pl.ds(0, n_chan - 1)]
+        return pltpu.make_async_remote_copy(
+            others, others, s_plane, r_plane, device_id={"chan": chan ^ 1}
+        )
 
     def halos(c):
         @pl.when(chan > 0)
@@ -263,7 +329,7 @@
             to_left(c).wait_recv()
 
     def relay_far():
-        pl.loop(RELAY, cables)(halos)
+        pl.loop(FAR_AT * CABLES, cables)(halos)
         inner = left[:1]
         for c in range(cables):
             last = slice(times - 1, times)
@@ -271,24 +337,24 @@
             far_send[cables + c : cables + c + 1, :] = jnp.where(inner, 0.0, halo_right[c, last, :])
         for_later(lambda d: far_to(d).start())
 
-    @pl.loop(0, cables)
-    def _(c):
-        @pl.when(c == RELAY)
-        def _():
-            relay_row()
-            relay_far()
-
-        @pl.when(c < RELAY)
-        def _():
-            halos(c)
-
-        def tile(buffer, i):
+    @pl.loop(0, cables // CABLES)
+    def _(k):
+        pl.when(k == FAR_AT)(relay_far)
+
+        @pl.when(k < FAR_AT)
+        def _():
+            for j in range(CABLES):
+                halos(k * CABLES + j)
+
+        def tile(buffer, c, i):
             return buffer[c, 8 * i : 8 * i + 8, :]
 
-        for at, low, high in ((0, halo_left, send_left), (blocks, send_right, halo_right)):
-            put(c, at, [jnp.where(left, tile(low, i), tile(high, i)) for i in range(8)])
+        for j in range(CABLES):
+            c = k * CABLES + j
+            for at, low, high in ((0, halo_left, send_left), (blocks, send_right, halo_right)):
+                put(c, at, [jnp.where(left, tile(low, c, i), tile(high, c, i)) for i in range(8)])
         pl.run_scoped(
-            lambda *acc: filtered(c, acc),
+            lambda *acc: filtered(k * CABLES, acc),
             *[pltpu.ACC(n % 2)((times, 2 * LANES), f32) for n in range(RING)],
         )
 
@@ -362,13 +428,24 @@
     common_out[...] = jnp.broadcast_to(row, (LANES, LANES)).T[:times]
 
 
-def final_kernel(y, offset, edge, common, out):
-    c = pl.program_id(0)
-    mode = common[...]
-    for j in range(out.shape[2] // LANES):
-        col = slice(j * LANES, (j + 1) * LANES)
-        shift = offset[c, j : j + 1, :] - mode * edge[c, j : j + 1, :]
-        out[0, :, col] = y[c, :, col] + shift
+def final_kernel(y, offset, edge, common, out, buffer, sem):
+    cables, _, width = y.shape
+
+    def copy(c):
+        return pltpu.make_async_copy(buffer.at[c], out.at[c], sem.at[c])
+
+    @pl.loop(0, cables)
+    def _(c):
+        mode = common[...]
+        for j in range(width // LANES):
+            col = slice(j * LANES, (j + 1) * LANES)
+            shift = offset[c, j : j + 1, :] - mode * edge[c, j : j + 1, :]
+            buffer[c, :, col] = y[c, :, col] + shift
+        copy(c).start()
+
+    @pl.loop(0, cables)
+    def _(c):
+        copy(c).wait()
 
 
 def shards(phase_step, wrap_count, coupling, filter_taps):
@@ -403,9 +480,9 @@
         ),
         scratch_shapes=[
             vmem(wide, f32), vmem(wide, jnp.int32), vmem(z, bf16), vmem(z, bf16),
-            [vmem((200, LANES), f32)] * GROUP, [vmem((200, LANES), f32)] * GROUP, vmem((times, LANES), f32),
+            [vmem((200, LANES), f32)] * (blocks + 1), [vmem((200, LANES), f32)] * (blocks + 1),
             vmem((cables, 2 * LANES, 2 * LANES), bf16),
-            vmem((times, LANES), f32), vmem((cables, blocks + 8, LANES), f32),
+            vmem((times, LANES), f32), vmem((times, LANES), f32), vmem((cables, blocks + 8, LANES), f32),
             vmem(edge, f32), vmem(edge, f32),
             vmem((cables, times, LANES), f32), vmem((cables, times, LANES), f32),
             vmem((n_tm, cables, blocks + 8, LANES), f32),
@@ -425,10 +502,10 @@
     )(phase_step, wrap_count, coupling, filter_taps)
     return pl.pallas_call(
         final_kernel,
-        grid=(cables,),
         out_shape=jax.ShapeDtypeStruct(full, f32),
         in_specs=[pl.BlockSpec(memory_space=vmem)] * 4,
-        out_specs=pl.BlockSpec((1, times, width), lambda c: (c, 0, 0)),
+        out_specs=pl.BlockSpec(memory_space=pl.ANY),
+        scratch_shapes=[vmem(full, f32), dma((cables,))],
         compiler_params=pltpu.CompilerParams(vmem_limit_bytes=16 << 20),
         name="finish",
     )(*[pltpu.with_memory_space_constraint(x, vmem) for x in leveled])

time: 27.7 us -> 21.6 us (0.78)
  Pallas kernels: 27.5 us -> 21.4 us
    pallas_call x1, Pallas kernels: 22.8 us -> 17.9 us  [shards(): pl.pallas_call(functools.partial(main_kernel, n_tm, n_chan), out_shape=(v...]
    pallas_call x1, Pallas kernels: 4.73 us -> 3.49 us  [shards(): pl.pallas_call(final_kernel, out_shape=jax.ShapeDtypeStruct(full, f32), i...]
where the time goes in v3:
time: 21.6 us; the launch traced here: 21.4 us
  Pallas kernels  21.4 us (99%)
    pallas_call x1, Pallas kernels, shards(): pl.pallas_call(functools.partial(main_kernel, n_tm, n_chan), out_shape=(v...  17.9 us
    pallas_call x1, Pallas kernels, shards(): pl.pallas_call(final_kernel, out_shape=jax.ShapeDtypeStruct(full, f32), i...  3.49 us

profile of v3, /device:TPU:1, one launch (start us, length us, event | category | flops | bytes accessed | tf_op | source)
XLA Modules:
  0.0 21.4 jit_solution(1890192900935120271)
XLA Ops:
  0.0 17.9 %level.1 = (f32[8,64,4096]{2,1,0:T(8,128)S(1)}, f32[8,32,128]{2,1,0:T(8,128)S(1)}, f32[8,32,128]{2,1,0:T(8,128)S(1)}, f32[64,128]{1,0:T(8,128)S(1)}) custom-call(f32[8,64,4096]{2,1,0:T(8,128)} %phase.1, s32[8,64,4096]{2,1,0:T(8,128)} %wrap.1, f32[8]{0:T(128)} %coupling.1, f32[8,128]{1,0:T(8,128)} %taps.1), custom_call_target="tpu_custom_call" | custom-call | tf_op jit(solution)/shard_map/level/pallas_call | solution.py:461
  17.9 3.5 %finish.1 = f32[8,64,4096]{2,1,0:T(8,128)} custom-call(f32[8,64,4096]{2,1,0:T(8,128)S(1)} %get-tuple-element.9.y, f32[8,32,128]{2,1,0:T(8,128)S(1)} %get-tuple-element.10.offset, f32[8,32,128]{2,1,0:T(8,128)S(1)} %get-tuple-element.11.edge, f32[64,128]{1,0:T(8,128)S(1)} %get-tuple-element.12.common), custom_call_target="tpu_custom_call" | custom-call | tf_op jit(solution)/shard_map/finish/pallas_call | solution.py:503

commit v4 on v3

--- a/solution.py
+++ b/solution.py
@@ -14,8 +14,8 @@
 RING = 8
 CABLES = 2
 DEFER = 4
-RELAY = 2
-FAR_AT = 1
+EARLY = 2
+RELAY = 1
 FIRST = 20
 LIMIT = 48
 f32 = jnp.float32
@@ -43,7 +43,7 @@
     phase, wrap, coupling, taps,
     ybuf, offset_out, edge_out, common_out,
     pbuf, wbuf, zhi, zlo, swap_in, swap_out, matrix, sums, late, ends,
-    send_left, send_right, halo_left, halo_right,
+    send_left, send_right, packed_left, packed_right, halo_left, halo_right,
     ends_in, far_send, far_in, own_row, row_in, plane_row, plane_in,
     sem_in, s_left, s_right, r_left, r_right,
     s_ends, r_ends, s_far, r_far, s_row, r_row, s_plane, r_plane,
@@ -93,7 +93,6 @@
     sublane = lax.broadcasted_iota(jnp.int32, (8, LANES), 0)
     left = lax.broadcasted_iota(jnp.int32, (8, LANES), 1) < LANES // 2
     sums[...] = jnp.zeros_like(sums)
-    ends[:, blocks:, :] = jnp.zeros((cables, 8, LANES), f32)
 
     @pl.when(chan == 0)
     def _():
@@ -105,13 +104,13 @@
 
     def to_left(c):
         return pltpu.make_async_remote_copy(
-            send_left.at[c], halo_right.at[c], s_left.at[c], r_right.at[c],
+            packed_left.at[c], halo_right.at[c], s_left.at[c], r_right.at[c],
             device_id={"chan": chan - 1},
         )
 
     def to_right(c):
         return pltpu.make_async_remote_copy(
-            send_right.at[c], halo_left.at[c], s_right.at[c], r_left.at[c],
+            packed_right.at[c], halo_left.at[c], s_right.at[c], r_left.at[c],
             device_id={"chan": chan + 1},
         )
 
@@ -171,13 +170,23 @@
             if b == edge:
                 for i, row in enumerate(rows):
                     buffer[c, 8 * i : 8 * i + 8, :] = row
+                for i in range(4):
+                    at = slice(8 * i, 8 * i + 8)
+                    late_rows = turn(rows[i + 4])
+                    if edge:
+                        packed_right[c, at, :] = jnp.where(left, rows[i], late_rows)
+                    else:
+                        packed_left[c, at, :] = jnp.where(left, late_rows, rows[i])
 
     def collect(c, b, total):
         rows = scanned(b)
         if total is not None:
             for i, row in enumerate(rows):
                 total[i] = total[i] + row
-        ends[c, b : b + 1, :] = rows[-1][7:8, :]
+        last = rows[-1][7:8, :]
+        if b == blocks:
+            last = jnp.where(left[:1], last, ends[c, 0:1, :])
+        ends[c, b % blocks : b % blocks + 1, :] = last
         if total is not None:
             keep_edge(c, b, rows)
         put(c, b, rows)
@@ -236,6 +245,7 @@
     pl.semaphore_wait(barrier, n_chan - 1 + n_tm - 1)
 
     pl.loop(0, cables - DEFER)(send_edges)
+    pl.loop(0, EARLY)(send_ends)
 
     late[...] = jnp.zeros_like(late)
 
@@ -255,7 +265,7 @@
     both = jnp.concatenate([sums[...], jnp.zeros_like(sums)], axis=0)
     own_row[...] = jnp.sum(both.T, axis=0, keepdims=True)
     for_later(lambda d: row_to(d).start())
-    pl.loop(0, cables - DEFER)(send_ends)
+    pl.loop(EARLY, cables - DEFER)(send_ends)
 
     def to_plane(d):
         return pltpu.make_async_remote_copy(
@@ -273,12 +283,6 @@
         for d in range(1, n_chan):
             to_plane(d ^ FIRST if d != FIRST else FIRST).start()
 
-    @pl.loop(cables - DEFER, cables)
-    def _(c):
-        pl.when(c == cables - DEFER + RELAY)(relay_row)
-        accumulate(c, ready=True)
-        send_ends(c)
-
     def window(z, c, w):
         return jnp.concatenate(
             [jnp.concatenate([z[c, i, w], z[c, i, w + 1]], axis=1) for i in range(parts)],
@@ -293,8 +297,8 @@
         pair = pltpu.matmul_pop(acc)
         return pair[:, :LANES] + pair[:, LANES:]
 
-    def filtered(first, acc):
-        order = [*range(1, blocks - 1), 0, blocks - 1]
+    def filtered(first, acc, outer):
+        order = [*range(1, blocks - 1)] + [0, blocks - 1] * outer
         work = [(first + k, w, n, k) for k in range(CABLES) for n, w in enumerate(order)]
 
         def finish(m):
@@ -329,34 +333,48 @@
             to_left(c).wait_recv()
 
     def relay_far():
-        pl.loop(FAR_AT * CABLES, cables)(halos)
-        inner = left[:1]
-        for c in range(cables):
-            last = slice(times - 1, times)
-            far_send[c : c + 1, :] = jnp.where(inner, halo_left[c, last, :], 0.0)
-            far_send[cables + c : cables + c + 1, :] = jnp.where(inner, 0.0, halo_right[c, last, :])
+        pl.loop(0, cables)(halos)
+        last = slice(times // 2 - 1, times // 2)
+        halo_rows = [halo[c, last, :] for halo in (halo_left, halo_right) for c in range(cables)]
+        halo_rows = turn(jnp.concatenate(halo_rows, axis=0))
+        from_left = lax.broadcasted_iota(jnp.int32, halo_rows.shape, 0) < cables
+        low = lax.broadcasted_iota(jnp.int32, halo_rows.shape, 1) < LANES // 2
+        far_send[...] = jnp.where(from_left == low, halo_rows, 0.0)
         for_later(lambda d: far_to(d).start())
 
-    @pl.loop(0, cables // CABLES)
-    def _(k):
-        pl.when(k == FAR_AT)(relay_far)
-
-        @pl.when(k < FAR_AT)
-        def _():
-            for j in range(CABLES):
-                halos(k * CABLES + j)
-
+    def edge_blocks(k):
         def tile(buffer, c, i):
-            return buffer[c, 8 * i : 8 * i + 8, :]
-
-        for j in range(CABLES):
-            c = k * CABLES + j
+            if buffer is send_left or buffer is send_right:
+                return buffer[c, 8 * i : 8 * i + 8, :]
+            packed = buffer[c, 8 * (i % 4) : 8 * (i % 4) + 8, :]
+            return packed if i < 4 else turn(packed)
+
+        for c in (k * CABLES + j for j in range(CABLES)):
             for at, low, high in ((0, halo_left, send_left), (blocks, send_right, halo_right)):
                 put(c, at, [jnp.where(left, tile(low, c, i), tile(high, c, i)) for i in range(8)])
-        pl.run_scoped(
-            lambda *acc: filtered(k * CABLES, acc),
-            *[pltpu.ACC(n % 2)((times, 2 * LANES), f32) for n in range(RING)],
-        )
+
+    def matmuls(body):
+        pl.run_scoped(body, *[pltpu.ACC(n % 2)((times, 2 * LANES), f32) for n in range(RING)])
+
+    @pl.loop(0, DEFER // CABLES)
+    def _(k):
+        pl.when(k == jnp.where(tm == 0, 0, RELAY))(relay_row)
+
+        def body(*acc):
+            filtered(k * CABLES, acc, False)
+            for j in range(CABLES):
+                accumulate(cables - DEFER + k * CABLES + j, ready=True)
+
+        matmuls(body)
+        for j in range(CABLES):
+            send_ends(cables - DEFER + k * CABLES + j)
+
+    relay_far()
+
+    @pl.loop(DEFER // CABLES, cables // CABLES)
+    def _(k):
+        edge_blocks(k)
+        matmuls(lambda *acc: filtered(k * CABLES, acc, True))
 
     from_earlier(lambda d: ends_to(d, ends, ends_in.at[tm]).wait_recv())
     from_earlier(lambda d: far_to(d).wait_recv())
@@ -364,9 +382,8 @@
     for source in range(n_tm - 1):
         far = far + jnp.where(source < tm, far_in[source], 0.0)
 
-    padded = blocks + 8
-    row_of = lax.broadcasted_iota(jnp.int32, (padded, LANES), 0)
-    position = row_of[:blocks]
+    position = lax.broadcasted_iota(jnp.int32, (blocks, LANES), 0)
+    low_half = lax.broadcasted_iota(jnp.int32, (blocks, LANES), 1) < LANES // 2
     ones = jnp.ones((16, LANES), f32)
     which = lax.broadcasted_iota(jnp.int32, (16, LANES), 0)
     half = lax.broadcasted_iota(jnp.int32, (16, LANES), 1) < LANES // 2
@@ -378,21 +395,35 @@
         axis=1,
     )
 
+    for k in range(DEFER // CABLES):
+        edge_blocks(k)
+
     def constants(*accs):
+        outer = accs[2 * cables :]
         for c in range(cables):
             mxu, small, constant = c % 2, accs[2 * c], accs[2 * c + 1]
-            here = jnp.zeros((padded, LANES), f32)
+            own = jnp.zeros((blocks, LANES), f32)
             for source in range(n_tm - 1):
-                here = here + jnp.where(source < tm, ends_in[source, c], 0.0)
-            here = here + jnp.where(row_of == 0, far[c : c + 1, :], 0.0)
-            here = here + jnp.where(row_of == blocks, far[cables + c : cables + c + 1, :], 0.0)
-            after = pltpu.roll(here, padded - 1, 0)[:blocks]
+                own = own + jnp.where(source < tm, ends_in[source, c], 0.0)
+            here = jnp.where((position == 0) & low_half, far[c : c + 1, :], own)
+            after = jnp.where(
+                (position == blocks - 1) & ~low_half,
+                far[cables + c : cables + c + 1, :],
+                pltpu.roll(own, blocks - 1, 0),
+            )
             pltpu.matmul_push_rhs(matrix[c], 0, mxu, transpose=True)
-            for i, pair in enumerate(zip(halves(here[:blocks]), halves(after))):
+            for i, pair in enumerate(zip(halves(here), halves(after))):
                 pltpu.matmul_acc_lhs(small, jnp.concatenate(pair, axis=1), None if i else 0)
             pltpu.matmul_acc_lhs(constant, one_rows)
+            if c < DEFER:
+                for acc, w in zip(outer[2 * c :], (0, blocks - 1)):
+                    pltpu.matmul_acc_lhs(acc, window(zhi, c, w))
+                    pltpu.matmul_acc_lhs(acc, window(zlo, c, w))
         for c in range(cables):
             offset_out[c] = joined(accs[2 * c])
+            if c < DEFER:
+                for acc, w in zip(outer[2 * c :], (0, blocks - 1)):
+                    ybuf[c, :, w * LANES : (w + 1) * LANES] = joined(acc)
             flat = joined(accs[2 * c + 1]) * coupling[c]
             edge = jnp.broadcast_to(flat[0:1, :], (blocks, LANES))
             edge = jnp.where((position == 0) & (chan == 0), flat[1:2, :], edge)
@@ -406,6 +437,7 @@
             for c in range(cables)
             for size in (blocks, 16)
         ],
+        *[pltpu.ACC(c % 2)((times, 2 * LANES), f32) for c in range(DEFER) for _ in range(2)],
     )
 
     for_later(lambda d: row_to(d).wait_send())
@@ -482,10 +514,10 @@
             vmem(wide, f32), vmem(wide, jnp.int32), vmem(z, bf16), vmem(z, bf16),
             [vmem((200, LANES), f32)] * (blocks + 1), [vmem((200, LANES), f32)] * (blocks + 1),
             vmem((cables, 2 * LANES, 2 * LANES), bf16),
-            vmem((times, LANES), f32), vmem((times, LANES), f32), vmem((cables, blocks + 8, LANES), f32),
+            vmem((times, LANES), f32), vmem((times, LANES), f32), vmem((cables, blocks, LANES), f32),
             vmem(edge, f32), vmem(edge, f32),
-            vmem((cables, times, LANES), f32), vmem((cables, times, LANES), f32),
-            vmem((n_tm, cables, blocks + 8, LANES), f32),
+            *[vmem((cables, times // 2, LANES), f32)] * 4,
+            vmem((n_tm, cables, blocks, LANES), f32),
             vmem((2 * cables, LANES), f32), vmem((n_tm, 2 * cables, LANES), f32),
             vmem((1, LANES), f32), vmem((n_tm, 1, LANES), f32),
             vmem((1, LANES), f32), vmem((n_chan, 1, LANES), f32),

time: 21.6 us -> 20.7 us (0.958)
  the two profiles are of different devices: /device:TPU:1 before, /device:TPU:96 now
where the time goes in v4:
time: 20.7 us; the launch traced here: 20.6 us
  Pallas kernels  20.6 us (100%)
    pallas_call x1, Pallas kernels, shards(): pl.pallas_call(functools.partial(main_kernel, n_tm, n_chan), out_shape=(v...  17.1 us
    pallas_call x1, Pallas kernels, shards(): pl.pallas_call(final_kernel, out_shape=jax.ShapeDtypeStruct(full, f32), i...  3.49 us

profile of v4, /device:TPU:96, one launch (start us, length us, event | category | flops | bytes accessed | tf_op | source)
XLA Modules:
  0.0 20.6 jit_solution(11945756217579313932)
XLA Ops:
  0.0 17.1 %level.1 = (f32[8,64,4096]{2,1,0:T(8,128)S(1)}, f32[8,32,128]{2,1,0:T(8,128)S(1)}, f32[8,32,128]{2,1,0:T(8,128)S(1)}, f32[64,128]{1,0:T(8,128)S(1)}) custom-call(f32[8,64,4096]{2,1,0:T(8,128)} %phase.1, s32[8,64,4096]{2,1,0:T(8,128)} %wrap.1, f32[8]{0:T(128)} %coupling.1, f32[8,128]{1,0:T(8,128)} %taps.1), custom_call_target="tpu_custom_call" | custom-call | tf_op jit(solution)/shard_map/level/pallas_call | solution.py:493
  17.1 3.5 %finish.1 = f32[8,64,4096]{2,1,0:T(8,128)} custom-call(f32[8,64,4096]{2,1,0:T(8,128)S(1)} %get-tuple-element.9.y, f32[8,32,128]{2,1,0:T(8,128)S(1)} %get-tuple-element.10.offset, f32[8,32,128]{2,1,0:T(8,128)S(1)} %get-tuple-element.11.edge, f32[64,128]{1,0:T(8,128)S(1)} %get-tuple-element.12.common), custom_call_target="tpu_custom_call" | custom-call | tf_op jit(solution)/shard_map/finish/pallas_call | solution.py:535

commit v5 on v4

--- a/solution.py
+++ b/solution.py
@@ -16,7 +16,6 @@
 DEFER = 4
 EARLY = 2
 RELAY = 1
-FIRST = 20
 LIMIT = 48
 f32 = jnp.float32
 bf16 = jnp.bfloat16
@@ -280,8 +279,8 @@
             row = row + jnp.where(source < tm, last, 0.0)
         plane_row[...] = row
         plane_in[chan] = row
-        for d in range(1, n_chan):
-            to_plane(d ^ FIRST if d != FIRST else FIRST).start()
+        for d in sorted(range(1, n_chan), key=lambda d: -((d >> 4 & 1) + (d >> 2 & 1))):
+            to_plane(d).start()
 
     def window(z, c, w):
         return jnp.concatenate(

time: 20.7 us -> 20.7 us (level)
  no operation moved by 1% of the time
where the time goes in v5:
time: 20.7 us; the launch traced here: 20.5 us
  Pallas kernels  20.5 us (99%)
    pallas_call x1, Pallas kernels, shards(): pl.pallas_call(functools.partial(main_kernel, n_tm, n_chan), out_shape=(v...  17 us
    pallas_call x1, Pallas kernels, shards(): pl.pallas_call(final_kernel, out_shape=jax.ShapeDtypeStruct(full, f32), i...  3.49 us

profile of v5, /device:TPU:96, one launch (start us, length us, event | category | flops | bytes accessed | tf_op | source)
XLA Modules:
  0.0 20.5 jit_solution(8203816352254434943)
XLA Ops:
  0.0 17.0 %level.1 = (f32[8,64,4096]{2,1,0:T(8,128)S(1)}, f32[8,32,128]{2,1,0:T(8,128)S(1)}, f32[8,32,128]{2,1,0:T(8,128)S(1)}, f32[64,128]{1,0:T(8,128)S(1)}) custom-call(f32[8,64,4096]{2,1,0:T(8,128)} %phase.1, s32[8,64,4096]{2,1,0:T(8,128)} %wrap.1, f32[8]{0:T(128)} %coupling.1, f32[8,128]{1,0:T(8,128)} %taps.1), custom_call_target="tpu_custom_call" | custom-call | tf_op jit(solution)/shard_map/level/pallas_call | solution.py:492
  17.0 3.5 %finish.1 = f32[8,64,4096]{2,1,0:T(8,128)} custom-call(f32[8,64,4096]{2,1,0:T(8,128)S(1)} %get-tuple-element.9.y, f32[8,32,128]{2,1,0:T(8,128)S(1)} %get-tuple-element.10.offset, f32[8,32,128]{2,1,0:T(8,128)S(1)} %get-tuple-element.11.edge, f32[64,128]{1,0:T(8,128)S(1)} %get-tuple-element.12.common), custom_call_target="tpu_custom_call" | custom-call | tf_op jit(solution)/shard_map/finish/pallas_call | solution.py:534
